TPU v7x, 1024 devices: a whole 4x8x16 slice. The times are simulated.
1024 devices in a mesh: fsdp: 16 (over y, core), tile: 64 (over x, z).
Axes of the slice: x: 4, y: 8, z: 16, core: 2. Of those that a mesh axis runs over, the one named last changes fastest.
Arguments:
- tiles: bfloat16 [16, 16384, 768], P('fsdp', 'tile')
- nbr_tiles: int32 [16, 4096, 4], P('fsdp', 'tile'), may hold values from 0 to 16383, as said below
- nbr_mask: int32 [16, 4096, 4], P('fsdp', 'tile'), may hold values 0 or 1
- tile_count: int32 [16], P('fsdp'), may hold values from 8192 to 16384, as said below
- w_query: bfloat16 [768, 768], P('fsdp'), may hold values from -0.21875 to 0.21875
- w_key: bfloat16 [768, 768], P('fsdp'), may hold values from -0.21875 to 0.21875
- w_value: bfloat16 [768, 768], P('fsdp'), may hold values from -0.21875 to 0.21875
- w_out: bfloat16 [768, 768], P('fsdp'), may hold values from -0.875 to 0.875
- key_gain: float32 [768], replicated, may hold values from 0.1 to 1.9
Outputs:
- attended: bfloat16 [16, 16384, 768], P('fsdp', 'tile')
Inputs may be any that keep to these rules, and one draw needn't show every extreme that they name: `nbr_tiles`: the slots of region r hold tiles with indices from (r // 64 - 1) * 256 to (r // 64 + 2) * 256 - 1, within the group. `tile_count`: some group has all 16384 tiles live.
All inputs are finite; a program needn't handle non-finite values. No bound on the sum of `nbr_mask` on one device may be relied on, other than what follows from the above.
Results may differ from a plain program's by a relative error of at most 0.008.
The roundings to bfloat16 on the way count: a program that leaves them out, or rounds other values in their place, can miss the bound.
Values may be sent and summed in bfloat16 or wider, within the bound.
A program may use at most 32 MiB of HBM per device.

v0:
```python
import jax
import jax.numpy as jnp
from jax import lax
from jax.sharding import PartitionSpec as P

HEADS = 16
NB = 4
REGIONS_PER_KEY = 8
KEY_DILATION = 2


def padded_2(cells, sides, width):
    for axis, dim in sides:
        count = lax.axis_size(axis)
        ends = count - 1
        head = lax.slice_in_dim(cells, 0, width, axis=dim)
        tail = lax.slice_in_dim(cells, cells.shape[dim] - width, cells.shape[dim], axis=dim)
        cells = jnp.concatenate(
            [
                lax.ppermute(tail, axis, [(i, (i + 1) % count) for i in range(ends)]),
                cells,
                lax.ppermute(head, axis, [((i + 1) % count, i) for i in range(ends)]),
            ],
            axis=dim,
        )
    return cells


def project_all(sources, w_query, w_key, w_value):
    pieces = (
        lax.all_gather(w_query, "fsdp", axis=0, tiled=True),
        lax.all_gather(w_key, "fsdp", axis=0, tiled=True),
        lax.all_gather(w_value, "fsdp", axis=0, tiled=True),
    )
    sums = tuple(
        (
            jnp.dot(src, key_segment, preferred_element_type=jnp.float32)
            for src, key_segment in zip(sources, pieces)
        )
    )
    return tuple((s.astype(jnp.bfloat16) for s in sums))


def by_parity(key_segment, head_list, window_width):
    region_number = key_segment.shape[0]
    split_point = key_segment.reshape(
        region_number // KEY_DILATION,
        KEY_DILATION,
        head_list // KEY_DILATION,
        KEY_DILATION,
        window_width,
    )
    selected_keys = jnp.stack(
        [
            split_point[:, inner_position, :, inner_position, :]
            for inner_position in range(KEY_DILATION)
        ],
        axis=2,
    )
    return selected_keys.reshape(region_number // KEY_DILATION, head_list, window_width)


def attend_block(state, key_piece, value_piece, query_heads, key_count_total):
    top, total, accum = state
    head_list = query_heads.shape[1]
    window_width = query_heads.shape[2]
    region_number = key_piece.shape[0]
    key_heads = by_parity(key_piece, head_list, window_width)
    value_heads = by_parity(value_piece, head_list, window_width)
    score = jnp.einsum(
        "qhd,khd->hqk", query_heads, key_heads, preferred_element_type=jnp.float32
    ) / jnp.sqrt(jnp.float32(window_width))
    pair_position = jnp.arange(region_number // KEY_DILATION, dtype=jnp.int32)
    head_position = jnp.arange(head_list, dtype=jnp.int32)
    key_position = KEY_DILATION * pair_position[None, :] + (head_position % KEY_DILATION)[:, None]
    valid_mask = key_position * 4 * REGIONS_PER_KEY < key_count_total
    score = jnp.where(valid_mask[:, None, :], score, -jnp.inf)
    new_top = jnp.maximum(top, jnp.max(score, axis=2))
    expo = jnp.exp(score - new_top[:, :, None])
    total = jnp.sum(expo, axis=2)
    accum = jnp.einsum(
        "hqk,khd->hqd", expo.astype(jnp.bfloat16), value_heads, preferred_element_type=jnp.float32
    )
    return (new_top, total, accum)


def body(tiles, nbr_tiles, nbr_mask, tile_count, w_query, w_key, w_value, w_out, key_gain):
    own_tiles = tiles[0]
    tile_rows, window_width = own_tiles.shape
    head_list = HEADS
    head_size = window_width // head_list
    device = lax.axis_index("tile")
    region_count = nbr_tiles.shape[1]
    key_rows = region_count // REGIONS_PER_KEY
    padded = padded_2(tiles, (("tile", 1),), tile_rows)[0]
    local_index = nbr_tiles[0] - (device - 1) * tile_rows
    rows = (
        jnp.take(padded, local_index.reshape(-1), axis=0)
        .reshape(region_count, NB, window_width)
        .astype(jnp.float32)
    )
    mask_f = nbr_mask[0].astype(jnp.float32)
    denom = jnp.maximum(jnp.sum(mask_f, axis=1), 1.0)
    region = jnp.sum(rows * mask_f[:, :, None], axis=1) / denom[:, None]
    pooled = jnp.mean(region.reshape(key_rows, REGIONS_PER_KEY, window_width), axis=1)
    normed = (
        pooled
        * lax.rsqrt(jnp.mean(pooled * pooled, axis=1, keepdims=True) + 1e-06)
        * key_gain[None, :]
    ).astype(jnp.bfloat16)
    key_count_total = tile_count[0]
    blank = (
        jnp.full((head_list, tile_rows), -1e30, jnp.float32),
        jnp.zeros((head_list, tile_rows), jnp.float32),
        jnp.zeros((head_list, tile_rows, head_size), jnp.float32),
    )
    query, keys, values = project_all((own_tiles, normed, normed), w_query, w_key, w_value)
    query_heads = query.reshape(tile_rows, head_list, head_size)
    top, total, accum = attend_block(
        blank,
        lax.all_gather(keys, "tile", axis=0, tiled=True),
        lax.all_gather(values, "tile", axis=0, tiled=True),
        query_heads,
        key_count_total,
    )
    context = accum / total[:, :, None]
    context = (
        jnp.transpose(context, (1, 0, 2)).reshape(tile_rows, window_width).astype(jnp.bfloat16)
    )
    attended = jnp.dot(
        context,
        lax.all_gather(w_out, "fsdp", axis=0, tiled=True),
        preferred_element_type=jnp.float32,
    )
    return attended.astype(jnp.bfloat16)[None]


def solution(mesh):
    placed = (
        P("fsdp", "tile", None),
        P("fsdp", "tile", None),
        P("fsdp", "tile", None),
        P("fsdp"),
        P("fsdp", None),
        P("fsdp", None),
        P("fsdp", None),
        P("fsdp", None),
        P(),
    )
    return jax.shard_map(
        body, mesh=mesh, in_specs=placed, out_specs=P("fsdp", "tile", None), check_vma=False
    )
```

profile of v0, /device:TPU:24, one launch (start us, length us, event | category | flops | bytes accessed | tf_op | source)
XLA Modules:
  0.0 304.1 jit_solution(10866186005731977017)
XLA Ops:
  6.5 0.7 all-gather.9.cloned.1.call-update
  7.3 0.7 all-gather.5.cloned.1.call-update
  8.1 0.7 all-gather.7.cloned.1.call-update
  8.8 1.3 collective-permute-start.1
  10.1 4.9 %collective-permute-start = (bf16[1,256,768]{2,1,0:T(8,128)(2,1)}, bf16[1,256,768]{2,1,0:T(8,128)(2,1)S(1)}, u32[]{:S(2)}, u32[]{:S(2)}) collective-permute-start(bf16[1,256,768]{2,1,0:T(8,128)(2,1)} %param.9), channel_id=1, source_target_pairs={{0,1},{1,2},{2,3},{3,4},{4,5},{5,6},{6,7},{7,8},{8,9},{9,10},{10,1... | collective-permute-start | bytes 1179656 | tf_op jit(solution)/shard_map/ppermute | solution.py:20
  15.1 0.7 convert_bitcast_fusion
  15.7 0.7 convert_reduce_fusion
  16.5 0.7 compare_and_fusion
  18.4 4.0 %collective-permute-done.1 = bf16[1,256,768]{2,1,0:T(8,128)(2,1)S(1)} collective-permute-done((bf16[1,256,768]{2,1,0:T(8,128)(2,1)}, bf16[1,256,768]{2,1,0:T(8,128)(2,1)S(1)}, u32[]{:S(2)}, u32[]{:S(2)}) %collective-permute-start.1) | collective-permute-done | bytes 393248 | tf_op jit(solution)/shard_map/ppermute | solution.py:22
  22.4 1.3 collective-permute-done
  23.7 1.1 maximum_bitcast_fusion
  24.8 1.2 gather_fusion
  26.1 0.6 multiply_reduce_fusion
  27.0 36.9 %all-gather.9.cloned.1.call-done = bf16[768,768]{1,0:T(8,128)(2,1)} async-done(((bf16[48,768]{1,0:T(8,128)(2,1)}), bf16[768,768]{1,0:T(8,128)(2,1)}) %all-gather.9.cloned.1.call-update) | async-done | bytes 1179664 | tf_op jit(solution)/shard_map/all_gather | solution.py:33
  63.8 1.6 convolution_convert_fusion.2
  65.4 103.2 %all_gather.22 = bf16[512,768]{1,0:T(8,128)(2,1)S(1)} all-gather(bf16[8,768]{1,0:T(8,128)(2,1)S(1)} %convolution_convert_fusion.2), channel_id=1, replica_groups=mesh['fsdp'=16,'tile'=64] {'tile'}, dimensions={0}, use_global_device_ids=true | all-gather | bytes 798720 | tf_op jit(solution)/shard_map/all_gather | solution.py:122
  168.6 2.5 reshape.129
  171.1 2.6 fusion.21
  173.8 3.4 %copy.45 = bf16[256,1,8,1,48]{0,4,3,2,1:T(8,128)(2,1)} copy(bf16[256,1,8,1,48]{4,3,2,1,0:T(2,128)(2,1)} %get-tuple-element.10) | data formatting | bytes 393216 | tf_op jit(solution)/shard_map/slice | solution.py:55
  177.2 1.8 copy.44
  179.0 1.7 convolution_convert_fusion.1
  180.8 0.2 copy.38
  181.0 1.6 convolution_convert_fusion.3
  182.6 98.8 %all_gather.20 = bf16[512,768]{1,0:T(8,128)(2,1)S(1)} all-gather(bf16[8,768]{1,0:T(8,128)(2,1)S(1)} %convolution_convert_fusion.3), channel_id=1, replica_groups=mesh['fsdp'=16,'tile'=64] {'tile'}, dimensions={0}, use_global_device_ids=true | all-gather | bytes 798720 | tf_op jit(solution)/shard_map/all_gather | solution.py:121
  281.4 2.5 reshape.127
  283.9 2.6 fusion.20
  286.5 2.3 copy.43
  288.8 0.8 copy.42
  289.8 2.4 fusion
  292.2 1.1 fusion.1
  293.3 1.7 fusion.13
  295.1 2.5 fusion.9
  (38 shorter events, 1.2 us)
Async XLA Ops:
  6.5 57.3 %all-gather.9.cloned.1.call-start = ((), (), s32[]{:S(2)}) async-start(), calls=%async_computation.2 | async-start | bytes 1253376 | tf_op jit(solution)/shard_map/all_gather | solution.py:33
  7.3 171.7 %all-gather.5.cloned.1.call-start = ((), (), s32[]{:S(2)}) async-start(), calls=%async_computation | async-start | bytes 1253376 | tf_op jit(solution)/shard_map/all_gather | solution.py:31
  8.0 173.0 %all-gather.7.cloned.1.call-start = ((), (), s32[]{:S(2)}) async-start(), calls=%async_computation.1 | async-start | bytes 1253376 | tf_op jit(solution)/shard_map/all_gather | solution.py:32
  8.7 286.3 %all-gather.11.cloned.1.call-start = ((), (), s32[]{:S(2)}) async-start(), calls=%async_computation.3 | async-start | bytes 1253376 | tf_op jit(solution)/shard_map/all_gather | solution.py:132
  8.8 13.6 %collective-permute-start.1 = (bf16[1,256,768]{2,1,0:T(8,128)(2,1)}, bf16[1,256,768]{2,1,0:T(8,128)(2,1)S(1)}, u32[]{:S(2)}, u32[]{:S(2)}) collective-permute-start(bf16[1,256,768]{2,1,0:T(8,128)(2,1)} %param.9), channel_id=1, source_target_pairs={{1,0},{2,1},{3,2},{4,3},{5,4},{6,5},{7,6},{8,7},{9,8},{10,9},{11,1... | collective-permute-start | bytes 1179656 | tf_op jit(solution)/shard_map/ppermute | solution.py:22
  10.1 13.6 %collective-permute-start = (bf16[1,256,768]{2,1,0:T(8,128)(2,1)}, bf16[1,256,768]{2,1,0:T(8,128)(2,1)S(1)}, u32[]{:S(2)}, u32[]{:S(2)}) collective-permute-start(bf16[1,256,768]{2,1,0:T(8,128)(2,1)} %param.9), channel_id=1, source_target_pairs={{0,1},{1,2},{2,3},{3,4},{4,5},{5,6},{6,7},{7,8},{8,9},{9,10},{10,1... | collective-permute-start | bytes 1179656 | tf_op jit(solution)/shard_map/ppermute | solution.py:20
  24.7 39.1 %copy-start.5 = (f32[768]{0:T(1024)S(1)}, f32[768]{0:T(1024)}, u32[]{:S(2)}) copy-start(f32[768]{0:T(1024)} %param.17) | copy-start | bytes 9220
  26.8 37.0 %copy-start.3 = (f32[8,768]{1,0:T(8,128)}, f32[8,768]{1,0:T(8,128)S(1)}, u32[]{:S(2)}) copy-start(f32[8,768]{1,0:T(8,128)S(1)} %fusion.17) | copy-start | bytes 73732
  171.1 7.9 %copy-start = (bf16[1,256,768]{2,1,0:T(8,128)(2,1)S(1)}, bf16[1,256,768]{2,1,0:T(8,128)(2,1)}, u32[]{:S(2)}) copy-start(bf16[1,256,768]{2,1,0:T(8,128)(2,1)} %param.9) | copy-start | bytes 1179652
  173.8 7.2 %copy-start.4 = (f32[8,768]{1,0:T(8,128)S(1)}, f32[8,768]{1,0:T(8,128)}, u32[]{:S(2)}) copy-start(f32[8,768]{1,0:T(8,128)} %copy-done.3) | copy-start | bytes 73732
  286.5 3.1 %copy-start.1 = (bf16[256,1,8,1,48]{0,4,3,2,1:T(8,128)(2,1)S(1)}, bf16[256,1,8,1,48]{0,4,3,2,1:T(8,128)(2,1)}, u32[]{:S(2)}) copy-start(bf16[256,1,8,1,48]{0,4,3,2,1:T(8,128)(2,1)} %copy.45) | copy-start | bytes 589828
  286.5 3.1 %copy-start.2 = (bf16[256,1,8,1,48]{0,4,3,2,1:T(8,128)(2,1)S(1)}, bf16[256,1,8,1,48]{0,4,3,2,1:T(8,128)(2,1)}, u32[]{:S(2)}) copy-start(bf16[256,1,8,1,48]{0,4,3,2,1:T(8,128)(2,1)} %copy.44) | copy-start | bytes 589828
Sparse Core Ops, SparseCore 0:
  10.1 53.7 all-gather.8
  66.5 45.6 all-gather.4
  114.9 45.6 all-gather.6
  163.2 45.6 all-gather.10
where the time goes:
time: 305 us; the launch traced here: 304 us
  blocking collectives  202 us (66%)
  waiting for transfers between devices  44.3 us (15%)
  local copies, waits for them, and re-layouts  20.6 us (7%)
  between operations  14 us (5%)
  matrix products  11.6 us (4%)
  starting transfers between devices  6.34 us (2%)
  other arithmetic  5.35 us (2%)
    all_gather x1, blocking collectives, body(): lax.all_gather(values, 'tile', axis=0, tiled=True)  103 us
    all_gather x1, blocking collectives, body(): lax.all_gather(keys, 'tile', axis=0, tiled=True)  98.8 us
    all_gather x1, waiting for transfers between devices, project_all(): lax.all_gather(w_value, 'fsdp', axis=0, tiled=True)  36.9 us
    slice x6, local copies, waits for them, and re-layouts, by_parity(): split_point[:, inner_position, :, inner_position, :]  13.6 us
  transfers between devices with their start and end apart: 6, of which 3 were waited for; matrix products, arithmetic and copies ran while one was open for 12% of the time, Pallas kernels for 0%

commit v1 on v0

v1 whole, which is shorter than its diff:
```python
import functools
import math

import jax
import jax.numpy as jnp
from jax import lax
from jax.experimental import pallas as pl
from jax.experimental.pallas import tpu as pltpu
from jax.sharding import PartitionSpec as P

HEADS = 16
REGIONS_PER_KEY = 8
TILES_PER_KEY = 32
NZ = 16
MESH = pl.DeviceIdType.MESH
BF16 = jnp.bfloat16
F32 = jnp.float32
WINDOWS = ((0, 128), (0, 128), (0, 256), (128, 128), (128, 128), (128, 256), (256, 128), (256, 128))


def pooling_weights(idx, msk, base, rows):
    m = msk.astype(F32)
    share = m / jnp.maximum(jnp.sum(m, axis=0, keepdims=True), 1.0)
    at = idx - base
    slots, regions = idx.shape
    tile = lax.broadcasted_iota(jnp.int32, (rows, regions), 0)
    acc = jnp.zeros((rows, regions), F32)
    for s in range(slots):
        acc = acc + jnp.where(tile == at[s : s + 1, :], share[s : s + 1, :], 0.0)
    acc = acc.T
    keys = regions // REGIONS_PER_KEY
    return jnp.sum(acc.reshape(keys, REGIONS_PER_KEY, rows), axis=1) * (1.0 / REGIONS_PER_KEY)


def exact_dot(w, x):
    hi = w.astype(BF16)
    rest = w - hi.astype(F32)
    mid = rest.astype(BF16)
    low = (rest - mid.astype(F32)).astype(BF16)
    n = w.shape[0]
    parts = jnp.concatenate([hi.astype(F32), mid.astype(F32), low.astype(F32)], axis=0).astype(BF16)
    y = jnp.dot(parts, x, preferred_element_type=F32)
    return y[:n] + y[n : 2 * n] + y[2 * n :]


def kernel(
    ny, nx, nz,
    tiles_hbm, idx_ref, msk_ref, cnt_ref, wq_hbm, wk_hbm, wv_hbm, wo_hbm, gain_ref,
    out_ref,
    tiles_v, w_v, ng, nf, nidx, nmsk, pout, pin, qz, kk, vt, ctxt, wvt,
    loc_sem, halo_send, halo_recv, ring_send, ring_r, ring_l, pair_send, pair_recv, z_send, z_recv, x_send, x_recv,
):
    f = lax.axis_index("fsdp")
    t = lax.axis_index("tile")
    nt = nx * nz
    nf_dev = 2 * ny
    y = f // 2
    core = f % 2
    xx = t // nz
    zz = t % nz
    w_hbm = (wq_hbm, wk_hbm, wv_hbm, wo_hbm)
    sh = wq_hbm.shape[0]
    rows, width = tiles_hbm.shape
    hd = width // HEADS
    half = HEADS // 2
    bl = half * hd

    def at_y(d):
        return (((y + d + ny) % ny) * 2 + core, t)

    def at_z(d):
        return (f, xx * nz + (zz + d + nz) % nz)

    def at_x(d):
        return (f, ((xx + d + nx) % nx) * nz + zz)

    def at_t(d):
        return (f, (t + d + nt) % nt)

    pair = (y * 2 + 1 - core, t)

    barrier = pltpu.get_barrier_semaphore()
    peers = [at_t(1), at_t(-1), pair]
    peers += [at_y(d) for d in ((1, -1) if ny > 1 else ())]
    peers += [at_x(d) for d in range(1, nx)]
    peers += [at_z(d) for d in range(1, nz)]
    for p in peers:
        pl.semaphore_signal(barrier, inc=1, device_id=p, device_id_type=MESH)

    load = pltpu.make_async_copy(tiles_hbm, tiles_v, loc_sem.at[0])
    load.start()

    def own_rows(owner_y, owner_core):
        return pl.ds(pl.multiple_of((owner_y * 2 + owner_core) * sh, sh), sh)

    mine = own_rows(y, core)
    own_loads = [pltpu.make_async_copy(w_hbm[w], w_v.at[w, mine, :], loc_sem.at[1 + w]) for w in range(4)]
    for c in own_loads:
        c.start()

    base = t * rows
    own_w = pooling_weights(idx_ref[...], msk_ref[...], base, rows)
    load.wait()
    own_part = exact_dot(own_w, tiles_v[...])
    pl.semaphore_wait(barrier, len(peers))

    def remote(src, dst, send, recv, dev):
        return pltpu.make_async_remote_copy(
            src_ref=src, dst_ref=dst, send_sem=send, recv_sem=recv, device_id=dev, device_id_type=MESH
        )

    def arrived(dst, sem):
        pltpu.make_async_copy(dst, dst, sem).wait()

    halo = []
    for slot, d in ((0, 1), (1, -1)):
        halo.append(remote(idx_ref, nidx.at[slot], halo_send.at[0, slot], halo_recv.at[0, slot], at_t(d)))
        halo.append(remote(msk_ref, nmsk.at[slot], halo_send.at[1, slot], halo_recv.at[1, slot], at_t(d)))
    for c in halo:
        c.start()

    far = ny // 2
    steps_r = [(ny - 1) // 2 + (1 if ny % 2 == 0 and w % 2 == 0 else 0) for w in range(4)]
    steps_l = [(ny - 1) // 2 + (1 if ny % 2 == 0 and w % 2 == 1 else 0) for w in range(4)]
    if ny == 1:
        steps_r = steps_l = [0] * 4

    def slot_of(w, owner_d):
        return w_v.at[w, own_rows((y + owner_d + ny) % ny, core), :]

    def pass_on(w, owner_d):
        ref = w_hbm[w] if owner_d == 0 else slot_of(w, owner_d)
        remote(ref, slot_of(w, owner_d), pair_send.at[w], pair_recv.at[w], pair).start()

    def ring_start(w, s, right):
        d = -(s - 1) if right else s - 1
        ref = w_hbm[w] if s == 1 else slot_of(w, d)
        sem = (ring_r if right else ring_l).at[w, s - 1]
        remote(ref, slot_of(w, d), ring_send.at[w], sem, at_y(1 if right else -1)).start()

    def first(w):
        if steps_r[w] >= 1:
            ring_start(w, 1, True)
        if steps_l[w] >= 1:
            ring_start(w, 1, False)
        pass_on(w, 0)

    def relay(w, s):
        if steps_r[w] >= s:
            arrived(slot_of(w, -s), ring_r.at[w, s - 1])
            if steps_r[w] > s:
                ring_start(w, s + 1, True)
            pass_on(w, -s)
        if steps_l[w] >= s:
            arrived(slot_of(w, s), ring_l.at[w, s - 1])
            if steps_l[w] > s:
                ring_start(w, s + 1, False)
            pass_on(w, s)

    def complete(w):
        own_loads[w].wait()
        whole = w_v.at[w, pl.ds(0, ny * sh), :]
        arrived(whole, pair_recv.at[w])

    def partials():
        for slot, d in ((0, -1), (1, 1)):
            arrived(nidx.at[slot], halo_recv.at[0, slot])
            arrived(nmsk.at[slot], halo_recv.at[1, slot])
            wts = pooling_weights(nidx[slot], nmsk[slot], base, rows)
            pout[slot] = exact_dot(wts, tiles_v[...])
            remote(pout.at[slot], pin.at[1 - slot], halo_send.at[2, slot], halo_recv.at[2, 1 - slot], at_t(d)).start()

    def normed():
        for slot in (0, 1):
            arrived(pin.at[slot], halo_recv.at[2, slot])
        pooled = own_part + pin[0] + pin[1]
        scale = lax.rsqrt(jnp.mean(pooled * pooled, axis=1, keepdims=True) + 1e-06)
        ng[t] = (pooled * scale * gain_ref[...]).astype(BF16)
        for d in range(1, nz):
            e = (d + 1) // 2 if d % 2 else -(d // 2)
            e = e % nz
            remote(ng.at[t], ng.at[t], z_send, z_recv.at[e], at_z(e)).start()
        x_send_block(0)

    def x_send_block(e):
        src = xx * nz + (zz - e + nz) % nz
        for d in range(1, nx):
            remote(ng.at[src], ng.at[src], x_send, x_recv, at_x(d)).start()

    def z_arrival(e):
        src = xx * nz + (zz - e + nz) % nz
        arrived(ng.at[src], z_recv.at[e])
        x_send_block(e)

    def query():
        complete(0)
        q = jnp.dot(tiles_v[...], w_v[0], preferred_element_type=F32)
        qt = q.T.astype(BF16)
        qz[...] = jnp.zeros(qz.shape, BF16)
        for h in range(HEADS):
            g, i = divmod(h, half)
            lo = hd * i - WINDOWS[i][0]
            qz[g, i, lo : lo + hd, :] = qt[h * hd : (h + 1) * hd, :]

    def value_weights():
        complete(2)
        wvt[...] = w_v[2].T

    def gathered():
        if nx > 1:
            many = nz * (nx - 1)
            arrived(ng.at[pl.ds(0, many)], x_recv)
        every = ng[...].astype(F32).reshape(nf.shape[1], width)
        for j in range(nf.shape[0]):
            nf[j] = every[:, j * 128 : (j + 1) * 128]

    def keys_values():
        n_par = nf.shape[1] // 2
        for par in (0, 1):
            n = [nf[j, pl.ds(par, n_par, stride=2), :] for j in range(nf.shape[0])]
            n = jnp.concatenate(n, axis=1).astype(BF16)
            kk[par] = jnp.dot(n, w_v[1], preferred_element_type=F32).astype(BF16)
            vt[par] = lax.dot_general(
                wvt[...], n, (((1,), (1,)), ((), ())), preferred_element_type=F32
            ).astype(BF16)

    def attend():
        n_par = kk.shape[1]
        count = cnt_ref[0]
        factor = math.log2(math.e) / math.sqrt(hd)
        position = lax.broadcasted_iota(jnp.int32, (n_par, rows), 0) * (2 * TILES_PER_KEY)

        @pl.loop(0, 2)
        def _(g):
            for i in range(half):
                par = i % 2
                valid = position + par * TILES_PER_KEY < count
                lo, wide = WINDOWS[i]
                lanes = pl.ds(pl.multiple_of(g * bl + lo, 128), wide)
                score = jnp.dot(kk[par, :, lanes], qz[g, i, :wide, :], preferred_element_type=F32)
                score = jnp.where(valid, score, -jnp.inf)
                top = jnp.max(score, axis=0, keepdims=True)
                weight = jnp.exp2((score - top) * factor)
                total = jnp.sum(weight, axis=0, keepdims=True)
                head = pl.ds(pl.multiple_of(g * bl + i * hd, 16), hd)
                acc = jnp.dot(vt[par, head, :], weight.astype(BF16), preferred_element_type=F32)
                ctxt[head, :] = (acc / total).astype(BF16)

    def project():
        complete(3)
        out_ref[...] = jnp.dot(ctxt[...].T, w_v[3], preferred_element_type=F32).astype(BF16)

    events = []

    def ev(when, fn, *args):
        events.append((when, len(events), fn, args))

    ev(0.1, first, 0)
    ev(0.2, first, 1)
    ev(1.7, partials)
    ev(3.3, relay, 0, 1)
    ev(4.0, normed)
    ev(4.9, relay, 1, 1)
    ev(5.0, first, 2)
    ev(6.5, relay, 0, 2)
    ev(8.0, relay, 1, 2)
    ev(8.1, first, 3)
    ev(9.6, relay, 0, 3)
    ev(11.2, relay, 2, 1)
    ev(12.0, relay, 1, 3)
    ev(12.5, relay, 3, 1)
    ev(13.0, relay, 0, 4)
    ev(13.2, relay, 1, 4)
    ev(13.4, query)
    ev(15.0, relay, 2, 2)
    ev(15.6, relay, 3, 2)
    ev(18.0, relay, 2, 3)
    ev(18.5, relay, 3, 3)
    ev(20.0, relay, 2, 4)
    ev(20.5, relay, 3, 4)
    for d in range(1, nz):
        e = ((d + 1) // 2 if d % 2 else -(d // 2)) % nz
        ev(5.0 + 2.0 + 0.6 * d, z_arrival, e)
    ev(18.1, gathered)
    ev(18.2, complete, 1)
    ev(20.6, value_weights)
    ev(20.7, keys_values)
    ev(20.8, attend)
    ev(21.0, project)
    for _, _, fn, args in sorted(events, key=lambda e: e[:2]):
        fn(*args)

    for c in halo:
        c.wait_send()
    for slot in (0, 1):
        pltpu.make_async_copy(pout.at[slot], pout.at[slot], halo_send.at[2, slot]).wait()
    for w in range(4):
        arrived(w_v.at[w, pl.ds(0, ny * sh), :], pair_send.at[w])
        if ny > 1:
            arrived(w_v.at[w, pl.ds(0, (ny - 1) * sh), :], ring_send.at[w])
    arrived(ng.at[pl.ds(0, nz - 1)], z_send)
    if nx > 1:
        arrived(ng.at[pl.ds(0, nz * (nx - 1))], x_send)


def body(ny, nx, nz, tiles, nbr_tiles, nbr_mask, tile_count, w_query, w_key, w_value, w_out, key_gain):
    rows, width = tiles.shape[1:]
    idx = jnp.transpose(nbr_tiles[0])
    msk = jnp.transpose(nbr_mask[0])
    slots, regions = idx.shape
    keys_dev = regions // REGIONS_PER_KEY
    nt = nx * nz
    keys = keys_dev * nt
    any_space = pl.BlockSpec(memory_space=pl.ANY)
    vmem = pl.BlockSpec(memory_space=pltpu.VMEM)
    dma = pltpu.SemaphoreType.DMA
    out = pl.pallas_call(
        functools.partial(kernel, ny, nx, nz),
        out_shape=jax.ShapeDtypeStruct((rows, width), BF16),
        in_specs=[any_space, vmem, vmem, pl.BlockSpec(memory_space=pltpu.SMEM)] + [any_space] * 4 + [vmem],
        out_specs=vmem,
        scratch_shapes=[
            pltpu.VMEM((rows, width), BF16),
            pltpu.VMEM((4, width, width), BF16),
            pltpu.VMEM((nt, keys_dev, width), BF16),
            pltpu.VMEM((width // 128, keys, 128), F32),
            pltpu.VMEM((2, slots, regions), jnp.int32),
            pltpu.VMEM((2, slots, regions), jnp.int32),
            pltpu.VMEM((2, keys_dev, width), F32),
            pltpu.VMEM((2, keys_dev, width), F32),
            pltpu.VMEM((2, HEADS // 2, 256, rows), BF16),
            pltpu.VMEM((2, keys // 2, width), BF16),
            pltpu.VMEM((2, width, keys // 2), BF16),
            pltpu.VMEM((width, rows), BF16),
            pltpu.VMEM((width, width), BF16),
            dma((5,)),
            dma((3, 2)),
            dma((3, 2)),
            dma((4,)),
            dma((4, 4)),
            dma((4, 4)),
            dma((4,)),
            dma((4,)),
            dma,
            dma((nz,)),
            dma,
            dma,
        ],
        compiler_params=pltpu.CompilerParams(
            collective_id=0, has_side_effects=True, vmem_limit_bytes=56 * 1024 * 1024
        ),
        name="dilated_attention",
    )(tiles[0], idx, msk, tile_count, w_query, w_key, w_value, w_out, key_gain.reshape(1, width))
    return out[None]


def solution(mesh, nz=NZ):
    ny = mesh.shape["fsdp"] // 2
    nx = mesh.shape["tile"] // nz
    placed = (
        P("fsdp", "tile", None),
        P("fsdp", "tile", None),
        P("fsdp", "tile", None),
        P("fsdp"),
        P("fsdp", None),
        P("fsdp", None),
        P("fsdp", None),
        P("fsdp", None),
        P(),
    )
    return jax.shard_map(
        functools.partial(body, ny, nx, nz),
        mesh=mesh, in_specs=placed, out_specs=P("fsdp", "tile", None), check_vma=False,
    )
```

time: 305 us -> 66.4 us (0.22)
  the two profiles are of different devices: /device:TPU:24 before, /device:TPU:1 now
where the time goes in v1:
time: 66.4 us; the launch traced here: 66.1 us
  Pallas kernels  63.1 us (95%)
  local copies, waits for them, and re-layouts  2.37 us (4%)
  between operations  0.68 us (1%)
    pallas_call x1, Pallas kernels, body(): pl.pallas_call(functools.partial(kernel, ny, nx, nz), out_shape=jax.Shape...  63.1 us
    unnamed x3, local copies, waits for them, and re-layouts  1.79 us

profile of v1, /device:TPU:1, one launch (start us, length us, event | category | flops | bytes accessed | tf_op | source)
XLA Modules:
  0.0 66.1 jit_solution(1552664919319987899)
XLA Ops:
  0.0 0.0 copy-start
  0.7 0.0 copy-done
  0.7 0.6 reshape.3.gain_ref
  1.3 63.1 %dilated_attention.1 = bf16[256,768]{1,0:T(8,128)(2,1)} custom-call(bf16[256,768]{1,0:T(8,128)(2,1)} %bitcast.9, s32[4,64]{1,0:T(4,128)} %bitcast.10, s32[4,64]{1,0:T(4,128)} %bitcast.11, s32[1]{0:T(128)S(6)} %copy.11.cnt_ref, bf16[48,768]{1,0:T(8,128)(2,1)} %wq_hbm.1, bf16[48,768]{1,0:T(8,128)(2,1)} %wk_hbm.1, bf16[48,768]{1,0:T(8,128)(2,1)} %wv_hbm.1, ...), custom_call_target="tpu_custom_call" | custom-call | tf_op jit(solution)/shard_map/dilated_attention/pallas_call | solution.py:317
  64.4 1.8 %copy.12 = bf16[1,256,768]{2,1,0:T(8,128)(2,1)} copy(bf16[1,256,768]{2,1,0:T(8,128)(2,1)} %bitcast.8) | data formatting | bytes 786432
Async XLA Ops:
  0.0 0.7 %copy-start = (f32[768]{0:T(1024)S(1)}, f32[768]{0:T(1024)}, u32[]{:S(2)}) copy-start(f32[768]{0:T(1024)} %param.17) | copy-start | bytes 9220

commit v2 on v1

v2 whole, which is shorter than its diff:
```python
import functools
import math

import jax
import jax.numpy as jnp
from jax import lax
from jax.experimental import pallas as pl
from jax.experimental.pallas import tpu as pltpu
from jax.sharding import PartitionSpec as P

HEADS = 16
REGIONS_PER_KEY = 8
TILES_PER_KEY = 32
NZ = 16
MESH = pl.DeviceIdType.MESH
BF16 = jnp.bfloat16
GROUPS = ((0,), (1, 2, 3), (4, 5, 6, 7), (8, 9, 10, 11), (12, 13, 14), (15,))
F32 = jnp.float32
WINDOWS = ((0, 128), (0, 128), (0, 256), (128, 128), (128, 128), (128, 256), (256, 128), (256, 128))


def pooling_weights(idx, msk, base, rows):
    m = msk.astype(F32)
    share = m / jnp.maximum(jnp.sum(m, axis=0, keepdims=True), 1.0)
    at = idx - base
    slots, regions = idx.shape
    tile = lax.broadcasted_iota(jnp.int32, (rows, regions), 0)
    acc = jnp.zeros((rows, regions), F32)
    for s in range(slots):
        acc = acc + jnp.where(tile == at[s : s + 1, :], share[s : s + 1, :], 0.0)
    acc = acc.T
    keys = regions // REGIONS_PER_KEY
    return jnp.sum(acc.reshape(keys, REGIONS_PER_KEY, rows), axis=1) * (1.0 / REGIONS_PER_KEY)


def exact_dot(w, x):
    hi = w.astype(BF16)
    rest = w - hi.astype(F32)
    mid = rest.astype(BF16)
    low = (rest - mid.astype(F32)).astype(BF16)
    n = w.shape[0]
    parts = jnp.concatenate([hi.astype(F32), mid.astype(F32), low.astype(F32)], axis=0).astype(BF16)
    y = jnp.dot(parts, x, preferred_element_type=F32)
    return y[:n] + y[n : 2 * n] + y[2 * n :]


STARTS = (0.0, 2.6, 5.0, 5.2, 7.3, 8.8, 10.3, 10.0, 12.7, 12.7, 14.8, 15.7, 15.2, 16.2, 18.0, 15.9)
RELAYS = ((0, 1), (1, 1), (0, 2), (1, 2), (0, 3), (1, 3), (0, 4), (1, 4))


def chunks(nz):
    if nz == len(STARTS):
        return ((0, 1), (1, 5), (5, 9), (9, 13), (13, 16))
    return ((0, 1), (1, nz))


def expected(nz):
    start = [STARTS[z * (len(STARTS) - 1) // max(nz - 1, 1)] for z in range(nz)]

    def dist(a, b):
        d = abs(a - b)
        return min(d, nz - d)

    def data(d):
        return 0.9 + 0.77 * d

    def signal(d):
        return 0.25 + 0.7 * d

    ready = [max(start[max(z - 1, 0) : z + 2]) + 2.0 for z in range(nz)]
    up = ready
    last = nz - 1
    arrive = {}
    for z in range(nz):
        if z > 0:
            arrive[z, 0] = max(ready[z], ready[z - 1] + data(1))
        if z < last:
            arrive[z, 1] = max(ready[z], ready[z + 1] + data(1))
    arrive[0, 0] = up[last] + data(2)
    arrive[last, 1] = arrive[0, 0] + data(2)
    part = {k: v + 0.6 for k, v in arrive.items()}
    norm = []
    for z in range(nz):
        left = part[z - 1, 1] + data(1) if z > 0 else part[last, 1] + data(2)
        right = part[z + 1, 0] + data(1) if z < last else part[0, 0] + data(2)
        norm.append(max(left, right, up[z], part[z, 0], part[z, 1]) + 0.3)
    sent = {}
    for z in range(nz):
        for e in range(1, nz):
            to = z + e
            sent[z, e] = norm[z] if to >= nz else max(norm[z], up[to] + signal(dist(z, to)))
    plans = []
    for z in range(nz):
        p = [(arrive[z, 0], "part", 0), (arrive[z, 1], "part", 1), (norm[z], "norm", None)]
        for i, ws in enumerate(RELAYS):
            p.append((ready[z] + 1.7 + 3.4 * (i + 1 if i < 6 else 7), "relay", ws))
        for e in range(1, nz):
            if z + e < nz:
                p.append((sent[z, e], "zsend", z + e))
            src = (z - e) % nz
            p.append((sent[src, e] + data(dist(z, src)) + 0.3, "zarr", src))
        got = {src: tm for tm, kind, src in p if kind == "zarr"}
        got[z] = norm[z]
        for lo, hi in chunks(nz):
            p.append((max(got[src] for src in range(lo, hi)), "xsend", (lo, hi)))
        plans.append(p)
    return plans


def orders(nz):
    plans = expected(nz)
    groups = GROUPS if nz == len(STARTS) else tuple((z,) for z in range(nz))
    out = []
    for members in groups:
        when = {}
        for z in members:
            for tm, kind, arg in plans[z]:
                when[kind, arg] = max(tm, when.get((kind, arg), 0.0))
        done = when["norm", None]
        when = {k: max(tm, done + 0.01) if k[0] in ("zsend", "xsend") else tm for k, tm in when.items()}
        cuts = [-1.0] + [max(when["relay", (b, s)] for s in range(1, 5)) + 0.9 + b for b in (0, 1)] + [1e9]
        listed = sorted(when.items(), key=lambda it: it[1])
        stages = [[k for k, tm in listed if lo < tm <= hi] for lo, hi in zip(cuts[:-1], cuts[1:])]
        out.append((members, stages))
    return out


def kernel(
    ny, nx, nz,
    tiles_hbm, idx_hbm, msk_hbm, cnt_ref, wq_hbm, wk_hbm, wv_hbm, wo_hbm, gain_hbm,
    out_ref,
    tiles_v, w_v, ng, nf, oidx, omsk, ogain, nidx, nmsk, pown, pout, pin, qz, kk, vt, ctxt, wvt,
    loc_sem, halo_send, halo_recv, ring_send, ring_r, ring_l, pair_send, pair_recv, z_send, z_recv, x_send, x_recv,
    here_sem,
):
    f = lax.axis_index("fsdp")
    t = lax.axis_index("tile")
    nt = nx * nz
    y = f // 2
    core = f % 2
    xx = t // nz
    zz = t % nz
    w_hbm = (wq_hbm, wk_hbm, wv_hbm, wo_hbm)
    sh = wq_hbm.shape[0]
    rows, width = tiles_hbm.shape
    hd = width // HEADS
    half = HEADS // 2
    bl = half * hd

    def at_y(d):
        return (((y + d + ny) % ny) * 2 + core, t)

    def at_z(d):
        return (f, xx * nz + (zz + d + nz) % nz)

    def at_x(d):
        return (f, ((xx + d + nx) % nx) * nz + zz)

    def at_t(d):
        return (f, (t + d + nt) % nt)

    pair = (y * 2 + 1 - core, t)

    barrier = pltpu.get_barrier_semaphore()

    def greet(dev, sem=barrier):
        pl.semaphore_signal(sem, inc=1, device_id=dev, device_id_type=MESH)

    near = [pair]
    near += [at_y(d) for d in ((1, -1) if ny > 1 else ())]
    near += [at_x(d) for d in range(1, nx)]
    for p in near:
        greet(p)
    is_first = zz == 0
    is_last = zz == nz - 1

    @pl.when(jnp.logical_not(is_first))
    def _():
        greet(at_z(-1))

    @pl.when(is_first)
    def _():
        greet(at_t(-1))

    for k in range(1, nz):
        @pl.when(zz + k < nz)
        def _(k=k):
            greet(at_z(k))

    loads = [
        pltpu.make_async_copy(src, dst, loc_sem.at[i])
        for i, (src, dst) in enumerate(
            [(tiles_hbm, tiles_v), (idx_hbm, oidx), (msk_hbm, omsk), (gain_hbm, ogain)]
            + [(w_hbm[w], w_v.at[f, w]) for w in range(4)]
        )
    ]
    for c in loads:
        c.start()
    own_loads = loads[4:]
    pl.semaphore_wait(barrier, len(near) + zz + 1)

    def remote(src, dst, send, recv, dev):
        return pltpu.make_async_remote_copy(
            src_ref=src, dst_ref=dst, send_sem=send, recv_sem=recv, device_id=dev, device_id_type=MESH
        )

    def arrived(dst, sem):
        pltpu.make_async_copy(dst, dst, sem).wait()

    def lists_to(d):
        slot = 0 if d == 1 else 1
        remote(idx_hbm, nidx.at[slot], halo_send.at[0, slot], halo_recv.at[0, slot], at_t(d)).start()
        remote(msk_hbm, nmsk.at[slot], halo_send.at[1, slot], halo_recv.at[1, slot], at_t(d)).start()

    steps_r = [(ny - 1) // 2 + (1 if ny % 2 == 0 and b % 2 == 0 else 0) for b in range(2)]
    steps_l = [(ny - 1) // 2 + (1 if ny % 2 == 0 and b % 2 == 1 else 0) for b in range(2)]

    def slot_of(b, owner_d):
        return w_v.at[((y + owner_d + ny) % ny) * 2 + core, pl.ds(2 * b, 2)]

    def pass_on(b, owner_d):
        ref = slot_of(b, owner_d)
        remote(ref, ref, pair_send.at[b], pair_recv.at[b], pair).start()

    def ring_start(b, s, right):
        ref = slot_of(b, -(s - 1) if right else s - 1)
        sem = (ring_r if right else ring_l).at[b, s - 1]
        remote(ref, ref, ring_send.at[b], sem, at_y(1 if right else -1)).start()

    def relay(b, s):
        if steps_r[b] >= s:
            arrived(slot_of(b, -s), ring_r.at[b, s - 1])
            if steps_r[b] > s:
                ring_start(b, s + 1, True)
            pass_on(b, -s)
        if steps_l[b] >= s:
            arrived(slot_of(b, s), ring_l.at[b, s - 1])
            if steps_l[b] > s:
                ring_start(b, s + 1, False)
            pass_on(b, s)

    def complete(b):
        arrived(w_v.at[pl.ds(0, ny), pl.ds(2 * b, 2)], pair_recv.at[b])

    def weight(w):
        return w_v[:, w].reshape(width, width)

    lists_to(1)

    @pl.when(jnp.logical_not(is_first))
    def _():
        lists_to(-1)

    for k in range(1, nz):
        @pl.when(k <= zz)
        def _(k=k):
            greet(at_z(-k), here_sem.at[zz])

    for b in range(2):
        for c in own_loads[2 * b : 2 * b + 2]:
            c.wait()
        if steps_r[b] >= 1:
            ring_start(b, 1, True)
        if steps_l[b] >= 1:
            ring_start(b, 1, False)
    for b in range(2):
        pass_on(b, 0)

    base = t * rows
    for c in loads[:4]:
        c.wait()
    pown[...] = exact_dot(pooling_weights(oidx[...], omsk[...], base, rows), tiles_v[...])

    def part(slot):
        d = -1 if slot == 0 else 1
        arrived(nidx.at[slot], halo_recv.at[0, slot])
        arrived(nmsk.at[slot], halo_recv.at[1, slot])
        if slot == 0:
            @pl.when(is_first)
            def _():
                lists_to(-1)

        wts = pooling_weights(nidx[slot], nmsk[slot], base, rows)
        pout[slot] = exact_dot(wts, tiles_v[...])
        remote(pout.at[slot], pin.at[1 - slot], halo_send.at[2, slot], halo_recv.at[2, 1 - slot], at_t(d)).start()

    def norm():
        for slot in (0, 1):
            arrived(pin.at[slot], halo_recv.at[2, slot])
        pooled = pown[...] + pin[0] + pin[1]
        scale = lax.rsqrt(jnp.mean(pooled * pooled, axis=1, keepdims=True) + 1e-06)
        ng[t] = (pooled * scale * ogain[...].reshape(1, width)).astype(BF16)
        for d in range(1, nz):
            e = ((d + 1) // 2 if d % 2 else -(d // 2)) % nz

            @pl.when(zz + e >= nz)
            def _(e=e):
                z_block(zz + e - nz)


    def z_block(to):
        remote(ng.at[t], ng.at[t], z_send, z_recv.at[zz], (f, xx * nz + to)).start()

    def zsend(to):
        @pl.when(to > zz)
        def _():
            pl.semaphore_wait(here_sem.at[to], 1)
            z_block(to)

    def xsend(span):
        lo, hi = span
        block = ng.at[pl.ds(xx * nz + lo, hi - lo)]
        for d in range(1, nx):
            remote(block, block, x_send, x_recv, at_x(d)).start()

    def zarr(src):
        @pl.when(src != zz)
        def _():
            arrived(ng.at[xx * nz + src], z_recv.at[src])

    handlers = {
        "part": part, "norm": lambda _: norm(), "relay": lambda ws: relay(*ws),
        "zsend": zsend, "zarr": zarr, "xsend": xsend,
    }
    listed = orders(nz)

    def run(stage):
        for members, stages in listed:
            @pl.when(jnp.logical_and(zz >= members[0], zz <= members[-1]))
            def _(todo=stages[stage]):
                for kind, arg in todo:
                    handlers[kind](arg)

    def query():
        complete(0)
        q = jnp.dot(tiles_v[...], weight(0), preferred_element_type=F32)
        qt = q.T.astype(BF16)
        qz[...] = jnp.zeros(qz.shape, BF16)
        for h in range(HEADS):
            g, i = divmod(h, half)
            lo = hd * i - WINDOWS[i][0]
            qz[g, i, lo : lo + hd, :] = qt[h * hd : (h + 1) * hd, :]

    def value_weights():
        complete(1)
        wvt[...] = weight(2).T

    def gathered():
        if nx > 1:
            many = nz * (nx - 1)
            arrived(ng.at[pl.ds(0, many)], x_recv)
        every = ng[...].astype(F32).reshape(nf.shape[1], width)
        for j in range(nf.shape[0]):
            nf[j] = every[:, j * 128 : (j + 1) * 128]

    def keys_values():
        n_par = nf.shape[1] // 2
        for par in (0, 1):
            n = [nf[j, pl.ds(par, n_par, stride=2), :] for j in range(nf.shape[0])]
            n = jnp.concatenate(n, axis=1).astype(BF16)
            kk[par] = jnp.dot(n, weight(1), preferred_element_type=F32).astype(BF16)
            vt[par] = lax.dot_general(
                wvt[...], n, (((1,), (1,)), ((), ())), preferred_element_type=F32
            ).astype(BF16)

    def attend():
        n_par = kk.shape[1]
        count = cnt_ref[0]
        factor = math.log2(math.e) / math.sqrt(hd)
        position = lax.broadcasted_iota(jnp.int32, (n_par, rows), 0) * (2 * TILES_PER_KEY)

        @pl.loop(0, 2)
        def _(g):
            for i in range(half):
                par = i % 2
                valid = position + par * TILES_PER_KEY < count
                lo, wide = WINDOWS[i]
                lanes = pl.ds(pl.multiple_of(g * bl + lo, 128), wide)
                score = jnp.dot(kk[par, :, lanes], qz[g, i, :wide, :], preferred_element_type=F32)
                score = jnp.where(valid, score, -jnp.inf)
                top = jnp.max(score, axis=0, keepdims=True)
                weight = jnp.exp2((score - top) * factor)
                total = jnp.sum(weight, axis=0, keepdims=True)
                head = pl.ds(pl.multiple_of(g * bl + i * hd, 16), hd)
                acc = jnp.dot(vt[par, head, :], weight.astype(BF16), preferred_element_type=F32)
                ctxt[head, :] = (acc / total).astype(BF16)

    def project():
        out_ref[...] = jnp.dot(ctxt[...].T, weight(3), preferred_element_type=F32).astype(BF16)

    run(0)
    query()
    run(1)
    value_weights()
    run(2)
    gathered()
    keys_values()
    attend()
    project()

    for slot in (0, 1):
        arrived(nidx.at[slot], halo_send.at[0, slot])
        arrived(nmsk.at[slot], halo_send.at[1, slot])
        arrived(pout.at[slot], halo_send.at[2, slot])
    for b in range(2):
        arrived(w_v.at[pl.ds(0, ny), pl.ds(2 * b, 2)], pair_send.at[b])
        if ny > 1:
            arrived(w_v.at[pl.ds(0, ny - 1), pl.ds(2 * b, 2)], ring_send.at[b])
    arrived(ng.at[pl.ds(0, nz - 1)], z_send)
    if nx > 1:
        arrived(ng.at[pl.ds(0, nz * (nx - 1))], x_send)


def body(ny, nx, nz, tiles, nbr_tiles, nbr_mask, tile_count, w_query, w_key, w_value, w_out, key_gain):
    rows, width = tiles.shape[1:]
    idx = jnp.transpose(nbr_tiles[0])
    msk = jnp.transpose(nbr_mask[0])
    slots, regions = idx.shape
    keys_dev = regions // REGIONS_PER_KEY
    nt = nx * nz
    keys = keys_dev * nt
    any_space = pl.BlockSpec(memory_space=pl.ANY)
    vmem = pl.BlockSpec(memory_space=pltpu.VMEM)
    dma = pltpu.SemaphoreType.DMA
    out = pl.pallas_call(
        functools.partial(kernel, ny, nx, nz),
        out_shape=jax.ShapeDtypeStruct((rows, width), BF16),
        in_specs=[any_space] * 3 + [pl.BlockSpec(memory_space=pltpu.SMEM)] + [any_space] * 5,
        out_specs=vmem,
        scratch_shapes=[
            pltpu.VMEM((rows, width), BF16),
            pltpu.VMEM((2 * ny, 4, width // (2 * ny), width), BF16),
            pltpu.VMEM((nt, keys_dev, width), BF16),
            pltpu.VMEM((width // 128, keys, 128), F32),
            pltpu.VMEM((slots, regions), jnp.int32),
            pltpu.VMEM((slots, regions), jnp.int32),
            pltpu.VMEM((width,), F32),
            pltpu.VMEM((2, slots, regions), jnp.int32),
            pltpu.VMEM((2, slots, regions), jnp.int32),
            pltpu.VMEM((keys_dev, width), F32),
            pltpu.VMEM((2, keys_dev, width), F32),
            pltpu.VMEM((2, keys_dev, width), F32),
            pltpu.VMEM((2, HEADS // 2, 256, rows), BF16),
            pltpu.VMEM((2, keys // 2, width), BF16),
            pltpu.VMEM((2, width, keys // 2), BF16),
            pltpu.VMEM((width, rows), BF16),
            pltpu.VMEM((width, width), BF16),
            dma((8,)),
            dma((3, 2)),
            dma((3, 2)),
            dma((2,)),
            dma((2, 4)),
            dma((2, 4)),
            dma((2,)),
            dma((2,)),
            dma,
            dma((nz,)),
            dma,
            dma,
            pltpu.SemaphoreType.REGULAR((nz,)),
        ],
        compiler_params=pltpu.CompilerParams(
            collective_id=0, has_side_effects=True, vmem_limit_bytes=56 * 1024 * 1024
        ),
        name="dilated_attention",
    )(tiles[0], idx, msk, tile_count, w_query, w_key, w_value, w_out, key_gain)
    return out[None]


def solution(mesh, nz=NZ):
    ny = mesh.shape["fsdp"] // 2
    nx = mesh.shape["tile"] // nz
    placed = (
        P("fsdp", "tile", None),
        P("fsdp", "tile", None),
        P("fsdp", "tile", None),
        P("fsdp"),
        P("fsdp", None),
        P("fsdp", None),
        P("fsdp", None),
        P("fsdp", None),
        P(),
    )
    return jax.shard_map(
        functools.partial(body, ny, nx, nz),
        mesh=mesh, in_specs=placed, out_specs=P("fsdp", "tile", None), check_vma=False,
    )
```

time: 66.4 us -> 57.9 us (0.87)
  the two profiles are of different devices: /device:TPU:1 before, /device:TPU:2 now
where the time goes in v2:
time: 57.9 us; the launch traced here: 57.7 us
  Pallas kernels  55.2 us (95%)
  local copies, waits for them, and re-layouts  1.77 us (3%)
  between operations  0.66 us (1%)
    pallas_call x1, Pallas kernels, body(): pl.pallas_call(functools.partial(kernel, ny, nx, nz), out_shape=jax.Shape...  55.2 us
    unnamed x1, local copies, waits for them, and re-layouts  1.77 us

profile of v2, /device:TPU:2, one launch (start us, length us, event | category | flops | bytes accessed | tf_op | source)
XLA Modules:
  0.0 57.7 jit_solution(608460879215977483)
XLA Ops:
  0.7 55.2 %dilated_attention.1 = bf16[256,768]{1,0:T(8,128)(2,1)} custom-call(bf16[256,768]{1,0:T(8,128)(2,1)} %bitcast.9, s32[4,64]{1,0:T(4,128)} %bitcast.10, s32[4,64]{1,0:T(4,128)} %bitcast.11, s32[1]{0:T(128)S(6)} %copy.11.cnt_ref, bf16[48,768]{1,0:T(8,128)(2,1)} %wq_hbm.1, bf16[48,768]{1,0:T(8,128)(2,1)} %wk_hbm.1, bf16[48,768]{1,0:T(8,128)(2,1)} %wv_hbm.1, ...), custom_call_target="tpu_custom_call" | custom-call | tf_op jit(solution)/shard_map/dilated_attention/pallas_call | solution.py:425
  55.9 1.8 %copy.12 = bf16[1,256,768]{2,1,0:T(8,128)(2,1)} copy(bf16[1,256,768]{2,1,0:T(8,128)(2,1)} %bitcast.8) | data formatting | bytes 786432

commit v3 on v2

--- a/solution.py
+++ b/solution.py
@@ -45,6 +45,8 @@
 
 
 STARTS = (0.0, 2.6, 5.0, 5.2, 7.3, 8.8, 10.3, 10.0, 12.7, 12.7, 14.8, 15.7, 15.2, 16.2, 18.0, 15.9)
+LATE_RING = 13.0
+SLACK = 4.0
 RELAYS = ((0, 1), (1, 1), (0, 2), (1, 2), (0, 3), (1, 3), (0, 4), (1, 4))
 
 
@@ -54,7 +56,7 @@
     return ((0, 1), (1, nz))
 
 
-def expected(nz):
+def expected(nz, ring_from=0.0):
     start = [STARTS[z * (len(STARTS) - 1) // max(nz - 1, 1)] for z in range(nz)]
 
     def dist(a, b):
@@ -93,12 +95,15 @@
     for z in range(nz):
         p = [(arrive[z, 0], "part", 0), (arrive[z, 1], "part", 1), (norm[z], "norm", None)]
         for i, ws in enumerate(RELAYS):
-            p.append((ready[z] + 1.7 + 3.4 * (i + 1 if i < 6 else 7), "relay", ws))
+            pace = 2.2 if ring_from else 3.4
+            tm = max(ready[z], ring_from) + 1.7 + pace * (i + 1 if i < 6 else 7)
+            close = 1.5 if ring_from else 3.0
+            p.append((norm[z] + 1.1 + 0.01 * i if norm[z] - close < tm < norm[z] + 1.0 else tm, "relay", ws))
         for e in range(1, nz):
             if z + e < nz:
-                p.append((sent[z, e], "zsend", z + e))
+                p.append((sent[z, e] + 1.0, "zsend", z + e))
             src = (z - e) % nz
-            p.append((sent[src, e] + data(dist(z, src)) + 0.3, "zarr", src))
+            p.append((sent[src, e] + data(dist(z, src)) + SLACK, "zarr", src))
         got = {src: tm for tm, kind, src in p if kind == "zarr"}
         got[z] = norm[z]
         for lo, hi in chunks(nz):
@@ -108,21 +113,26 @@
 
 
 def orders(nz):
-    plans = expected(nz)
-    groups = GROUPS if nz == len(STARTS) else tuple((z,) for z in range(nz))
     out = []
-    for members in groups:
-        when = {}
-        for z in members:
-            for tm, kind, arg in plans[z]:
-                when[kind, arg] = max(tm, when.get((kind, arg), 0.0))
-        done = when["norm", None]
-        when = {k: max(tm, done + 0.01) if k[0] in ("zsend", "xsend") else tm for k, tm in when.items()}
-        cuts = [-1.0] + [max(when["relay", (b, s)] for s in range(1, 5)) + 0.9 + b for b in (0, 1)] + [1e9]
-        listed = sorted(when.items(), key=lambda it: it[1])
-        stages = [[k for k, tm in listed if lo < tm <= hi] for lo, hi in zip(cuts[:-1], cuts[1:])]
-        out.append((members, stages))
+    for members in GROUPS if nz == len(STARTS) else tuple((z,) for z in range(nz)):
+        if STARTS[members[0]] < LATE_RING:
+            out.append((members, (0,), order_of(members, expected(nz, LATE_RING))))
+            out.append((members, (1, 2, 3), order_of(members, expected(nz))))
+        else:
+            out.append((members, (0, 1, 2, 3), order_of(members, expected(nz))))
     return out
+
+
+def order_of(members, plans):
+    when = {}
+    for z in members:
+        for tm, kind, arg in plans[z]:
+            when[kind, arg] = max(tm, when.get((kind, arg), 0.0))
+    done = when["norm", None]
+    when = {k: max(tm, done + 0.01) if k[0] in ("zsend", "xsend") else tm for k, tm in when.items()}
+    cuts = [-1.0] + [max(when["relay", (b, s)] for s in range(1, 5)) + 0.9 + b for b in (0, 1)] + [1e9]
+    listed = sorted(when.items(), key=lambda it: it[1])
+    return [[k for k, tm in listed if lo < tm <= hi] for lo, hi in zip(cuts[:-1], cuts[1:])]
 
 
 def kernel(
@@ -325,8 +335,10 @@
     listed = orders(nz)
 
     def run(stage):
-        for members, stages in listed:
-            @pl.when(jnp.logical_and(zz >= members[0], zz <= members[-1]))
+        for members, columns, stages in listed:
+            rows_in = jnp.logical_and(zz >= members[0], zz <= members[-1])
+
+            @pl.when(jnp.logical_and(rows_in, jnp.logical_and(xx >= columns[0], xx <= columns[-1])))
             def _(todo=stages[stage]):
                 for kind, arg in todo:
                     handlers[kind](arg)
@@ -419,6 +431,7 @@
     keys_dev = regions // REGIONS_PER_KEY
     nt = nx * nz
     keys = keys_dev * nt
+    keep = functools.partial(pltpu.with_memory_space_constraint, memory_space=pltpu.HBM)
     any_space = pl.BlockSpec(memory_space=pl.ANY)
     vmem = pl.BlockSpec(memory_space=pltpu.VMEM)
     dma = pltpu.SemaphoreType.DMA
@@ -460,10 +473,10 @@
             pltpu.SemaphoreType.REGULAR((nz,)),
         ],
         compiler_params=pltpu.CompilerParams(
-            collective_id=0, has_side_effects=True, vmem_limit_bytes=56 * 1024 * 1024
+            collective_id=0, has_side_effects=True, vmem_limit_bytes=24 * 1024 * 1024
         ),
         name="dilated_attention",
-    )(tiles[0], idx, msk, tile_count, w_query, w_key, w_value, w_out, key_gain)
+    )(*(keep(a) for a in (tiles[0], idx, msk)), tile_count, *(keep(a) for a in (w_query, w_key, w_value, w_out, key_gain)))
     return out[None]
 
 

time: 57.9 us -> 55.7 us (0.962)
  the two profiles are of different devices: /device:TPU:2 before, /device:TPU:8 now
where the time goes in v3:
time: 55.7 us; the launch traced here: 55.5 us
  Pallas kernels  54.1 us (97%)
  local copies, waits for them, and re-layouts  0.75 us (1%)
  between operations  0.66 us (1%)
    pallas_call x1, Pallas kernels, body(): pl.pallas_call(functools.partial(kernel, ny, nx, nz), out_shape=jax.Shape...  54.1 us

profile of v3, /device:TPU:8, one launch (start us, length us, event | category | flops | bytes accessed | tf_op | source)
XLA Modules:
  0.0 55.5 jit_solution(12432921362389588103)
XLA Ops:
  0.7 54.1 %dilated_attention.1 = bf16[256,768]{1,0:T(8,128)(2,1)S(1)} custom-call(bf16[256,768]{1,0:T(8,128)(2,1)} %bitcast.9, s32[4,64]{1,0:T(4,128)} %bitcast.10, s32[4,64]{1,0:T(4,128)} %bitcast.11, s32[1]{0:T(128)S(6)} %copy.11.cnt_ref, bf16[48,768]{1,0:T(8,128)(2,1)} %wq_hbm.1, bf16[48,768]{1,0:T(8,128)(2,1)} %wk_hbm.1, bf16[48,768]{1,0:T(8,128)(2,1)} %wv_hbm.1, ...), custom_call_target="tpu_custom_call" | custom-call | tf_op jit(solution)/shard_map/dilated_attention/pallas_call | solution.py:438
  54.8 0.7 %copy.12 = bf16[1,256,768]{2,1,0:T(8,128)(2,1)} copy(bf16[1,256,768]{2,1,0:T(8,128)(2,1)S(1)} %bitcast.8) | data formatting | bytes 786432

commit v4 on v3

--- a/solution.py
+++ b/solution.py
@@ -53,7 +53,7 @@
 def chunks(nz):
     if nz == len(STARTS):
         return ((0, 1), (1, 5), (5, 9), (9, 13), (13, 16))
-    return ((0, 1), (1, nz))
+    return ((0, 1), (1, nz // 2 + 1), (nz // 2 + 1, nz))
 
 
 def expected(nz, ring_from=0.0):
@@ -95,9 +95,10 @@
     for z in range(nz):
         p = [(arrive[z, 0], "part", 0), (arrive[z, 1], "part", 1), (norm[z], "norm", None)]
         for i, ws in enumerate(RELAYS):
-            pace = 2.2 if ring_from else 3.4
+            alone = ring_from > 0.0 and z == 0
+            pace = 2.2 if alone else 3.4
             tm = max(ready[z], ring_from) + 1.7 + pace * (i + 1 if i < 6 else 7)
-            close = 1.5 if ring_from else 3.0
+            close = 1.5 if alone else 3.0
             p.append((norm[z] + 1.1 + 0.01 * i if norm[z] - close < tm < norm[z] + 1.0 else tm, "relay", ws))
         for e in range(1, nz):
             if z + e < nz:
@@ -123,6 +124,12 @@
     return out
 
 
+def in_first_half(kind, arg, nz):
+    if kind == "zarr":
+        return 1 <= arg <= nz // 2
+    return kind == "xsend" and 1 <= arg[0] and arg[1] <= nz // 2 + 1
+
+
 def order_of(members, plans):
     when = {}
     for z in members:
@@ -131,6 +138,8 @@
     done = when["norm", None]
     when = {k: max(tm, done + 0.01) if k[0] in ("zsend", "xsend") else tm for k, tm in when.items()}
     cuts = [-1.0] + [max(when["relay", (b, s)] for s in range(1, 5)) + 0.9 + b for b in (0, 1)] + [1e9]
+    first = [tm for (kind, arg), tm in when.items() if in_first_half(kind, arg, len(plans))]
+    cuts[2] = max([cuts[2]] + [tm + 0.001 for tm in first])
     listed = sorted(when.items(), key=lambda it: it[1])
     return [[k for k, tm in listed if lo < tm <= hi] for lo, hi in zip(cuts[:-1], cuts[1:])]
 
@@ -139,7 +148,7 @@
     ny, nx, nz,
     tiles_hbm, idx_hbm, msk_hbm, cnt_ref, wq_hbm, wk_hbm, wv_hbm, wo_hbm, gain_hbm,
     out_ref,
-    tiles_v, w_v, ng, nf, oidx, omsk, ogain, nidx, nmsk, pown, pout, pin, qz, kk, vt, ctxt, wvt,
+    tiles_v, w_v, ng, nf, oidx, omsk, ogain, nidx, nmsk, pown, pout, pin, qz, kk, vt, ctxt, wvt, tops, totals, accs,
     loc_sem, halo_send, halo_recv, ring_send, ring_r, ring_l, pair_send, pair_recv, z_send, z_recv, x_send, x_recv,
     here_sem,
 ):
@@ -321,7 +330,8 @@
         lo, hi = span
         block = ng.at[pl.ds(xx * nz + lo, hi - lo)]
         for d in range(1, nx):
-            remote(block, block, x_send, x_recv, at_x(d)).start()
+            sem = x_recv.at[0 if in_first_half("xsend", span, nz) else 1]
+            remote(block, block, x_send, sem, at_x(d)).start()
 
     def zarr(src):
         @pl.when(src != zz)
@@ -357,15 +367,17 @@
         complete(1)
         wvt[...] = weight(2).T
 
-    def gathered():
+    def attend(half_at):
+        rows_z = nz // 2
         if nx > 1:
-            many = nz * (nx - 1)
-            arrived(ng.at[pl.ds(0, many)], x_recv)
-        every = ng[...].astype(F32).reshape(nf.shape[1], width)
+            arrived(ng.at[pl.ds(0, rows_z * (nx - 1))], x_recv.at[half_at])
+        blocks = []
+        for x in range(nx):
+            at = x * nz
+            blocks += [ng[at + 1 : at + 1 + rows_z]] if half_at == 0 else [ng[at : at + 1], ng[at + 1 + rows_z : at + nz]]
+        every = jnp.concatenate([b.astype(F32).reshape(-1, width) for b in blocks], axis=0)
         for j in range(nf.shape[0]):
             nf[j] = every[:, j * 128 : (j + 1) * 128]
-
-    def keys_values():
         n_par = nf.shape[1] // 2
         for par in (0, 1):
             n = [nf[j, pl.ds(par, n_par, stride=2), :] for j in range(nf.shape[0])]
@@ -374,12 +386,17 @@
             vt[par] = lax.dot_general(
                 wvt[...], n, (((1,), (1,)), ((), ())), preferred_element_type=F32
             ).astype(BF16)
-
-    def attend():
-        n_par = kk.shape[1]
         count = cnt_ref[0]
         factor = math.log2(math.e) / math.sqrt(hd)
-        position = lax.broadcasted_iota(jnp.int32, (n_par, rows), 0) * (2 * TILES_PER_KEY)
+        at = lax.broadcasted_iota(jnp.int32, (n_par, rows), 0)
+        keys_z = ng.shape[1]
+        per_x = rows_z * keys_z // 2
+        within = 2 * (at % per_x)
+        if half_at == 0:
+            within = within + keys_z
+        else:
+            within = within + jnp.where(within >= keys_z, rows_z * keys_z, 0)
+        position = ((at // per_x) * (nz * keys_z) + within) * TILES_PER_KEY
 
         @pl.loop(0, 2)
         def _(g):
@@ -391,11 +408,22 @@
                 score = jnp.dot(kk[par, :, lanes], qz[g, i, :wide, :], preferred_element_type=F32)
                 score = jnp.where(valid, score, -jnp.inf)
                 top = jnp.max(score, axis=0, keepdims=True)
-                weight = jnp.exp2((score - top) * factor)
-                total = jnp.sum(weight, axis=0, keepdims=True)
+                weights = jnp.exp2((score - top) * factor)
+                total = jnp.sum(weights, axis=0, keepdims=True)
+                h = g * half + i
                 head = pl.ds(pl.multiple_of(g * bl + i * hd, 16), hd)
-                acc = jnp.dot(vt[par, head, :], weight.astype(BF16), preferred_element_type=F32)
-                ctxt[head, :] = (acc / total).astype(BF16)
+                acc = jnp.dot(vt[par, head, :], weights.astype(BF16), preferred_element_type=F32)
+                if half_at == 0:
+                    tops[h] = top
+                    totals[h] = total
+                    accs[head, :] = acc
+                else:
+                    old = tops[h]
+                    best = jnp.maximum(old, top)
+                    f_old = jnp.exp2((old - best) * factor)
+                    f_new = jnp.exp2((top - best) * factor)
+                    total = totals[h] * f_old + total * f_new
+                    ctxt[head, :] = ((accs[head, :] * f_old + acc * f_new) / total).astype(BF16)
 
     def project():
         out_ref[...] = jnp.dot(ctxt[...].T, weight(3), preferred_element_type=F32).astype(BF16)
@@ -404,10 +432,9 @@
     query()
     run(1)
     value_weights()
+    attend(0)
     run(2)
-    gathered()
-    keys_values()
-    attend()
+    attend(1)
     project()
 
     for slot in (0, 1):
@@ -444,7 +471,7 @@
             pltpu.VMEM((rows, width), BF16),
             pltpu.VMEM((2 * ny, 4, width // (2 * ny), width), BF16),
             pltpu.VMEM((nt, keys_dev, width), BF16),
-            pltpu.VMEM((width // 128, keys, 128), F32),
+            pltpu.VMEM((width // 128, keys // 2, 128), F32),
             pltpu.VMEM((slots, regions), jnp.int32),
             pltpu.VMEM((slots, regions), jnp.int32),
             pltpu.VMEM((width,), F32),
@@ -454,10 +481,13 @@
             pltpu.VMEM((2, keys_dev, width), F32),
             pltpu.VMEM((2, keys_dev, width), F32),
             pltpu.VMEM((2, HEADS // 2, 256, rows), BF16),
-            pltpu.VMEM((2, keys // 2, width), BF16),
-            pltpu.VMEM((2, width, keys // 2), BF16),
+            pltpu.VMEM((2, keys // 4, width), BF16),
+            pltpu.VMEM((2, width, keys // 4), BF16),
             pltpu.VMEM((width, rows), BF16),
             pltpu.VMEM((width, width), BF16),
+            pltpu.VMEM((HEADS, 1, rows), F32),
+            pltpu.VMEM((HEADS, 1, rows), F32),
+            pltpu.VMEM((width, rows), F32),
             dma((8,)),
             dma((3, 2)),
             dma((3, 2)),
@@ -469,7 +499,7 @@
             dma,
             dma((nz,)),
             dma,
-            dma,
+            dma((2,)),
             pltpu.SemaphoreType.REGULAR((nz,)),
         ],
         compiler_params=pltpu.CompilerParams(

time: 55.7 us -> 54.5 us (0.978)
  Pallas kernels: 54.1 us -> 52.9 us
    pallas_call x1, Pallas kernels: 54.1 us -> 52.9 us  [body(): pl.pallas_call(functools.partial(kernel, ny, nx, nz), out_shape=jax.Shape...]
where the time goes in v4:
time: 54.5 us; the launch traced here: 54.3 us
  Pallas kernels  52.9 us (97%)
  local copies, waits for them, and re-layouts  0.75 us (1%)
  between operations  0.66 us (1%)
    pallas_call x1, Pallas kernels, body(): pl.pallas_call(functools.partial(kernel, ny, nx, nz), out_shape=jax.Shape...  52.9 us

profile of v4, /device:TPU:8, one launch (start us, length us, event | category | flops | bytes accessed | tf_op | source)
XLA Modules:
  0.0 54.3 jit_solution(18085441418254954450)
XLA Ops:
  0.7 52.9 %dilated_attention.1 = bf16[256,768]{1,0:T(8,128)(2,1)S(1)} custom-call(bf16[256,768]{1,0:T(8,128)(2,1)} %bitcast.9, s32[4,64]{1,0:T(4,128)} %bitcast.10, s32[4,64]{1,0:T(4,128)} %bitcast.11, s32[1]{0:T(128)S(6)} %copy.11.cnt_ref, bf16[48,768]{1,0:T(8,128)(2,1)} %wq_hbm.1, bf16[48,768]{1,0:T(8,128)(2,1)} %wk_hbm.1, bf16[48,768]{1,0:T(8,128)(2,1)} %wv_hbm.1, ...), custom_call_target="tpu_custom_call" | custom-call | tf_op jit(solution)/shard_map/dilated_attention/pallas_call | solution.py:465
  53.6 0.7 %copy.12 = bf16[1,256,768]{2,1,0:T(8,128)(2,1)} copy(bf16[1,256,768]{2,1,0:T(8,128)(2,1)S(1)} %bitcast.8) | data formatting | bytes 786432

commit v5 on v4

--- a/solution.py
+++ b/solution.py
@@ -104,7 +104,7 @@
             if z + e < nz:
                 p.append((sent[z, e] + 1.0, "zsend", z + e))
             src = (z - e) % nz
-            p.append((sent[src, e] + data(dist(z, src)) + SLACK, "zarr", src))
+            p.append((sent[src, e] + data(dist(z, src)) + (SLACK if z > 7 else 5.5), "zarr", src))
         got = {src: tm for tm, kind, src in p if kind == "zarr"}
         got[z] = norm[z]
         for lo, hi in chunks(nz):

time: 54.5 us -> 60.9 us (1.12)
  the two profiles are of different devices: /device:TPU:8 before, /device:TPU:16 now
where the time goes in v5:
time: 60.9 us; the launch traced here: 60.7 us
  Pallas kernels  59.3 us (97%)
  local copies, waits for them, and re-layouts  0.75 us (1%)
  between operations  0.66 us (1%)
    pallas_call x1, Pallas kernels, body(): pl.pallas_call(functools.partial(kernel, ny, nx, nz), out_shape=jax.Shape...  59.3 us

profile of v5, /device:TPU:16, one launch (start us, length us, event | category | flops | bytes accessed | tf_op | source)
XLA Modules:
  0.0 60.7 jit_solution(10263896111321475925)
XLA Ops:
  0.7 59.3 %dilated_attention.1 = bf16[256,768]{1,0:T(8,128)(2,1)S(1)} custom-call(bf16[256,768]{1,0:T(8,128)(2,1)} %bitcast.9, s32[4,64]{1,0:T(4,128)} %bitcast.10, s32[4,64]{1,0:T(4,128)} %bitcast.11, s32[1]{0:T(128)S(6)} %copy.11.cnt_ref, bf16[48,768]{1,0:T(8,128)(2,1)} %wq_hbm.1, bf16[48,768]{1,0:T(8,128)(2,1)} %wk_hbm.1, bf16[48,768]{1,0:T(8,128)(2,1)} %wv_hbm.1, ...), custom_call_target="tpu_custom_call" | custom-call | tf_op jit(solution)/shard_map/dilated_attention/pallas_call | solution.py:465
  60.0 0.7 %copy.12 = bf16[1,256,768]{2,1,0:T(8,128)(2,1)} copy(bf16[1,256,768]{2,1,0:T(8,128)(2,1)S(1)} %bitcast.8) | data formatting | bytes 786432
